TPU v7x, 512 devices: a whole 4x4x16 slice. The times are simulated.
512 devices in a mesh: net: 16 (over z), seg: 8 (over y, core), corner: 4 (over x).
Axes of the slice: x: 4, y: 4, z: 16, core: 2. Of those that a mesh axis runs over, the one named last changes fastest.
Arguments:
- tile_values: bfloat16 [8192, 128, 1024], P(('net', 'seg', 'corner')), may hold values from -48 to 48
- tile_coords: int32 [8192, 3], P(('net', 'seg', 'corner')), may hold values from 0 to 511, as said below
- tile_count: int32 [512], P(('net', 'seg', 'corner')), may hold values from 12 to 16, as said below
- owner_map: int32 [512], P('net'), may hold values from 0 to 511, as said below
- corner_factor: bfloat16 [64, 256], P('corner')
- seg_factor: bfloat16 [65536, 256], P(('seg', 'net'))
Outputs:
- net_factor: float32 [65536, 256], P(('net', 'seg', 'corner'))
Inputs may be any that keep to these rules, and one draw needn't show every extreme that they name: `tile_coords`: row t of device d gives a corner block within the corner range stored by d's corner index, a net block that owner_map assigns to an owner slot of d's net index, and a segment block within the segment range of d's seg index. Among a device's 16 rows at most 2 name segment blocks stored by any one device of the net axis, and on every device two live rows name segment blocks stored by the same device of the net axis. The first tile_count[d] rows of device d are live; the others are ignored. `owner_map`: A permutation of the 512 net blocks.
All inputs are finite; a program needn't handle non-finite values.
Results may differ from a plain program's by a relative error of at most 0.0058.
The roundings to bfloat16 on the way count: a program that leaves them out, or rounds other values in their place, can miss the bound.
Values may be sent and summed in bfloat16 or wider, within the bound.
No kernel may reach another device: no remote copies, remote signals or barrier semaphores. Data moves between devices by JAX's collectives and lax.ppermute only.
A program may use at most 64 MiB of HBM per device.

v0:
```python
import jax
import jax.numpy as jnp
from jax import lax
from jax.sharding import PartitionSpec as P

CBLK = 8
GRP = 4


def solve_rows(gram, mttkrp):
    cholesky_low = jnp.linalg.cholesky(gram)
    forward = lax.linalg.triangular_solve(cholesky_low, mttkrp.T, left_side=True, lower=True)
    backward = lax.linalg.triangular_solve(
        cholesky_low, forward, left_side=True, lower=True, transpose_a=True
    )
    return backward.T


def contract(packed):
    values, corner_rows, seg_rows = packed
    khatri = (
        corner_rows.astype(jnp.float32)[:, :, None, :] * seg_rows.astype(jnp.float32)[:, None, :, :]
    ).astype(jnp.bfloat16)
    khatri = khatri.reshape(values.shape[0], values.shape[2], corner_rows.shape[2])
    return jnp.einsum("tnj,tjr->tnr", values, khatri, preferred_element_type=jnp.float32)


def body(tile_values, tile_coords, tile_count, owner_map, corner_factor, seg_factor):
    slot_total = tile_values.shape[0]
    net_rows = tile_values.shape[1]
    columns = corner_factor.shape[1]
    seg_width = tile_values.shape[2] // CBLK
    held_blocks = seg_factor.shape[0] // seg_width
    net_devices = lax.axis_size("net")
    corner_local = tile_coords[:, 0] - lax.axis_index("corner") * (corner_factor.shape[0] // CBLK)
    seg_local = tile_coords[:, 2] - lax.axis_index("seg") * (held_blocks * net_devices)
    corner_sel = jnp.take(corner_factor.reshape(-1, CBLK, columns), corner_local, axis=0)
    gathered = lax.all_gather(seg_factor, "net", axis=0, tiled=True)
    seg_sel = jnp.take(gathered.reshape(-1, seg_width, columns), seg_local, axis=0)
    groups = slot_total // GRP
    partial_value = lax.map(
        contract,
        (
            tile_values.reshape(groups, GRP, net_rows, -1),
            corner_sel.reshape(groups, GRP, CBLK, columns),
            seg_sel.reshape(groups, GRP, seg_width, columns),
        ),
    )
    partial_value = partial_value.reshape(slot_total, net_rows * columns)
    live_mask = jnp.arange(slot_total, dtype=jnp.int32) < tile_count[0]
    member = ((tile_coords[:, 1][:, None] == owner_map[None, :]) & live_mask[:, None]).astype(
        jnp.float32
    )
    summed = jnp.dot(
        member.T, partial_value, precision=lax.Precision.HIGHEST, preferred_element_type=jnp.float32
    )
    mttkrp = lax.psum_scatter(
        summed.reshape(net_rows * lax.axis_size(("seg", "corner")), columns),
        ("seg", "corner"),
        scatter_dimension=0,
        tiled=True,
    )
    corner_part = jnp.dot(corner_factor.T, corner_factor, preferred_element_type=jnp.float32)
    seg_part = jnp.dot(seg_factor.T, seg_factor, preferred_element_type=jnp.float32)
    seg_gram = lax.psum(seg_part, ("net", "seg"))
    corner_gram = lax.psum(corner_part, "corner")
    return solve_rows(corner_gram * seg_gram, mttkrp)


def solution(mesh):
    return jax.shard_map(
        body,
        mesh=mesh,
        in_specs=(
            P(("net", "seg", "corner"), None, None),
            P(("net", "seg", "corner"), None),
            P(("net", "seg", "corner")),
            P("net"),
            P("corner", None),
            P(("seg", "net"), None),
        ),
        out_specs=P(("net", "seg", "corner"), None),
        check_vma=False,
    )
```

profile of v0, /device:TPU:8, one launch (start us, length us, event | category | flops | bytes accessed | tf_op | source)
XLA Modules:
  0.0 481.0 jit_solution(18225845388589294858)
XLA Ops:
  7.4 0.7 all-gather.2.cloned.1.call-update
  8.1 2.1 fusion.23
  10.3 1.0 fusion.22
  11.4 0.7 slice_bitcast_fusion.6
  12.1 0.8 and_reduce_fusion
  12.8 0.1 broadcast_in_dim.38
  12.9 0.1 broadcast_in_dim.41
  13.7 0.6 gather_fusion
  14.3 0.1 broadcast_select_fusion.1
  14.3 79.2 %all-gather.2.cloned.1.call-done = bf16[8192,256]{1,0:T(8,128)(2,1)} async-done(((bf16[512,256]{1,0:T(8,128)(2,1)}), bf16[8192,256]{1,0:T(8,128)(2,1)}) %all-gather.2.cloned.1.call-update) | async-done | bytes 4194320 | tf_op jit(solution)/shard_map/all_gather | solution.py:38
  93.5 2.8 gather_fusion.1
  96.4 0.2 broadcast_select_fusion
  96.5 12.6 %while.11 = (s32[]{:T(128)}, f32[4,4,128,256]{3,2,1,0:T(8,128)}, bf16[4,4,128,1024]{3,2,1,0:T(8,128)(2,1)}, bf16[4,4,8,256]{3,2,1,0:T(8,128)(2,1)S(1)}, bf16[4,4,128,256]{3,2,1,0:T(8,128)(2,1)S(1)}, /*index=5*/s32[]{:T(128)}) while((s32[]{:T(128)}, f32[4,4,128,256]{3,2,1,0:T(8,128)}, bf16[4,4,128,1024]{3,2,1,0:T(8,128)(2,1)}, ...), condition=%wide.region_7.8_spmd, body=%wide.region_6.7_spmd.sunk | while | flops 270671872 | bytes 7160917 | solution.py:41
  96.6 0.6 multiply_convert_fusion.2
  97.2 2.5 fusion.43
  99.7 0.6 multiply_convert_fusion.2
  100.3 2.5 fusion.43
  102.9 0.6 multiply_convert_fusion.2
  103.5 2.5 fusion.43
  106.0 0.6 multiply_convert_fusion.2
  106.6 2.5 fusion.43
  109.1 2.8 copy.13
  111.9 3.5 fusion.15
  115.5 4.9 %reshape.80 = f32[4096,256]{1,0:T(8,128)} reshape(f32[32,32768]{1,0:T(8,128)} %fusion.15) | data formatting | bytes 8388608 | tf_op jit(solution)/shard_map/reshape | solution.py:58
  120.4 232.0 %all-reduce.6.cloned.1.call-done = f32[256,256]{0,1:T(8,128)} async-done(((f32[256,256]{0,1:T(8,128)}), f32[256,256]{0,1:T(8,128)}) %all-reduce.6.cloned.1.call-update) | async-done | bytes 262160 | tf_op jit(solution)/shard_map/psum | solution.py:65
  352.4 56.2 %all-reduce.4.cloned.1.call-done = f32[256,256]{0,1:T(8,128)} async-done(((f32[256,256]{0,1:T(8,128)}), f32[256,256]{0,1:T(8,128)}) %all-reduce.4.cloned.1.call-update) | async-done | bytes 262160 | tf_op jit(solution)/shard_map/psum | solution.py:66
  408.6 1.1 mul.24
  409.6 0.1 copy.9
  409.8 11.7 %cholesky.50 = f32[128,128]{1,0:T(8,128)S(1)} custom-call(f32[128,128]{1,0:T(8,128)S(1)} %cholesky.118), custom_call_target="Cholesky" | custom-call | tf_op jit(solution)/shard_map/jit(cholesky)/cholesky | solution.py:11
  421.6 9.8 %custom-call.16 = f32[1,128,128]{1,2,0:T(8,128)S(1)} custom-call(f32[1,128,128]{2,1,0:T(8,128)S(1)} %get-tuple-element.68), custom_call_target="InvertDiagBlocksLowerTriangular" | custom-call | tf_op jit(solution)/shard_map/jit(cholesky)/cholesky | solution.py:11
  431.4 0.2 constant_dynamic-update-slice_fusion.1
  431.6 0.3 convolution_subtract_fusion.2
  431.9 11.7 %cholesky.105 = f32[128,128]{1,0:T(8,128)S(1)} custom-call(f32[128,128]{1,0:T(8,128)S(1)} %convolution_subtract_fusion.2), custom_call_target="Cholesky" | custom-call | tf_op jit(solution)/shard_map/jit(cholesky)/cholesky | solution.py:11
  443.7 0.7 compare_reduce_fusion
  445.6 0.1 triangular_solve.66
  445.7 3.9 while.12
  445.7 0.6 fusion.44
  446.3 1.3 bitcast_dynamic-update-slice_fusion.2
  447.7 0.6 fusion.44
  448.3 1.3 bitcast_dynamic-update-slice_fusion.2
  449.6 19.9 %custom-call.17 = f32[2,128,128]{1,2,0:T(8,128)S(1)} custom-call(f32[2,128,128]{2,1,0:T(8,128)S(1)} %get-tuple-element.40), custom_call_target="InvertDiagBlocksLowerTriangular" | custom-call | tf_op jit(solution)/shard_map/triangular_solve | solution.py:13
  469.5 1.1 fusion.5
  470.7 1.1 convolution_subtract_fusion.1
  471.8 0.3 fusion.12
  472.1 0.2 fusion.11
  472.3 0.3 convolution_subtract_fusion
  472.6 0.2 fusion.10
  472.8 0.8 copy.10
  (35 shorter events, 0.6 us)
Async XLA Ops:
  7.4 2.9 copy-start
  7.4 86.2 %all-gather.2.cloned.1.call-start = ((), (), s32[]{:S(2)}) async-start(), calls=%async_computation.3 | async-start | bytes 4456448 | tf_op jit(solution)/shard_map/all_gather | solution.py:38
  8.1 344.3 %all-reduce.6.cloned.1.call-start = ((), (), s32[]{:S(2)}) async-start(), calls=%async_computation.2 | async-start | bytes 524288 | tf_op jit(solution)/shard_map/psum | solution.py:65
  10.3 398.3 %all-reduce.4.cloned.1.call-start = ((), (), s32[]{:S(2)}) async-start(), calls=%async_computation.1 | async-start | bytes 524288 | tf_op jit(solution)/shard_map/psum | solution.py:66
  11.3 458.2 %reduce-scatter.2.cloned.1.call-start = ((), (), s32[]{:S(2)}) async-start(), calls=%async_computation.4 | async-start | bytes 4325376 | tf_op jit(solution)/shard_map/reduce_scatter | solution.py:57
  109.1 2.8 copy-start.1
Sparse Core Ops, SparseCore 0:
  10.3 83.2 all-gather.1
  120.5 101.2 reduce-scatter.1
Sparse Core Ops, SparseCore 1:
  12.4 339.9 all-reduce.5
  354.7 53.8 all-reduce.3
where the time goes:
time: 482 us; the launch traced here: 481 us
  waiting for transfers between devices  368 us (76%)
  other arithmetic  58.6 us (12%)
  matrix products  20.2 us (4%)
  between operations  17 us (4%)
  local copies, waits for them, and re-layouts  16.8 us (3%)
    psum x1, waiting for transfers between devices, body(): seg_gram = lax.psum(seg_part, ('net', 'seg'))  232 us
    all_gather x1, waiting for transfers between devices, body(): gathered = lax.all_gather(seg_factor, 'net', axis=0, tiled=True)  79.2 us
    psum x1, waiting for transfers between devices, body(): corner_gram = lax.psum(corner_part, 'corner')  56.2 us
    another operation x6, other arithmetic, solve_rows(): cholesky_low = jnp.linalg.cholesky(gram)  34 us
    another operation x3, other arithmetic, solve_rows(): lax.linalg.triangular_solve(cholesky_low, forward, left_side=True, lower=...  19.9 us
    dot_general x4, matrix products, contract(): jnp.einsum('tnj,tjr->tnr', values, khatri, preferred_element_type=jnp.flo...  9.96 us
  transfers between devices with their start and end apart: 4, of which 3 were waited for; matrix products, arithmetic and copies ran while one was open for 19% of the time, Pallas kernels for 0%

commit v1 on v0

--- a/solution.py
+++ b/solution.py
@@ -5,6 +5,11 @@
 
 CBLK = 8
 GRP = 4
+
+
+def gather_from_all(x, axis, dim):
+    copies = jnp.concatenate([x] * lax.axis_size(axis), axis=dim)
+    return lax.all_to_all(copies, axis, dim, dim, tiled=True)
 
 
 def solve_rows(gram, mttkrp):
@@ -35,7 +40,7 @@
     corner_local = tile_coords[:, 0] - lax.axis_index("corner") * (corner_factor.shape[0] // CBLK)
     seg_local = tile_coords[:, 2] - lax.axis_index("seg") * (held_blocks * net_devices)
     corner_sel = jnp.take(corner_factor.reshape(-1, CBLK, columns), corner_local, axis=0)
-    gathered = lax.all_gather(seg_factor, "net", axis=0, tiled=True)
+    gathered = gather_from_all(seg_factor, "net", 0)
     seg_sel = jnp.take(gathered.reshape(-1, seg_width, columns), seg_local, axis=0)
     groups = slot_total // GRP
     partial_value = lax.map(

time: 482 us -> 566 us (1.17)
  waiting for transfers between devices: 368 us -> 430 us
  starting transfers between devices: 0.13 us -> 15.5 us
  local copies, waits for them, and re-layouts: 16.8 us -> 26.1 us
    all_to_all x0 -> x1, waiting for transfers between devices: none -> 180 us  [gather_from_all(): return lax.all_to_all(copies, axis, dim, dim, tiled=True)]
    all_gather x1 -> x0, waiting for transfers between devices: 79.2 us -> none  [body(): gathered = lax.all_gather(seg_factor, 'net', axis=0, tiled=True)]
    psum x1, waiting for transfers between devices: 232 us -> 193 us  [body(): seg_gram = lax.psum(seg_part, ('net', 'seg'))]
    all_to_all x0 -> x1, starting transfers between devices: none -> 15.4 us  [gather_from_all(): return lax.all_to_all(copies, axis, dim, dim, tiled=True)]
    unnamed x5 -> x26, local copies, waits for them, and re-layouts: 2.84 us -> 12.8 us
  transfers between devices with their start and end apart: 4 -> 4, of which waited for: 3 -> 3; matrix products, arithmetic and copies ran while one was open for 19% -> 16% of each run, Pallas kernels for 0% -> 0%
where the time goes in v1:
time: 566 us; the launch traced here: 565 us
  waiting for transfers between devices  430 us (76%)
  other arithmetic  57.8 us (10%)
  local copies, waits for them, and re-layouts  26.1 us (5%)
  matrix products  19.2 us (3%)
  between operations  17.1 us (3%)
  starting transfers between devices  15.5 us (3%)
    psum x1, waiting for transfers between devices, body(): seg_gram = lax.psum(seg_part, ('net', 'seg'))  193 us
    all_to_all x1, waiting for transfers between devices, gather_from_all(): return lax.all_to_all(copies, axis, dim, dim, tiled=True)  180 us
    psum x1, waiting for transfers between devices, body(): corner_gram = lax.psum(corner_part, 'corner')  56.5 us
    another operation x6, other arithmetic, solve_rows(): cholesky_low = jnp.linalg.cholesky(gram)  34 us
    another operation x3, other arithmetic, solve_rows(): lax.linalg.triangular_solve(cholesky_low, forward, left_side=True, lower=...  19.9 us
    all_to_all x1, starting transfers between devices, gather_from_all(): return lax.all_to_all(copies, axis, dim, dim, tiled=True)  15.4 us
    unnamed x26, local copies, waits for them, and re-layouts  12.8 us
  transfers between devices with their start and end apart: 4, of which 3 were waited for; matrix products, arithmetic and copies ran while one was open for 16% of the time, Pallas kernels for 0%

profile of v1, /device:TPU:8, one launch (start us, length us, event | category | flops | bytes accessed | tf_op | source)
XLA Modules:
  0.0 565.3 jit_solution(1328085299285931321)
XLA Ops:
  7.4 1.0 constant_dynamic-update-slice_fusion.15
  8.4 1.0 constant_dynamic-update-slice_fusion.14
  9.4 1.0 constant_dynamic-update-slice_fusion.13
  10.4 1.0 constant_dynamic-update-slice_fusion.12
  11.3 1.0 constant_dynamic-update-slice_fusion.11
  12.3 1.0 constant_dynamic-update-slice_fusion.10
  13.3 1.0 constant_dynamic-update-slice_fusion.9
  14.3 1.0 constant_dynamic-update-slice_fusion.8
  15.5 2.0 copy-done.2
  17.4 15.4 %all-to-all-start = ((bf16[16,512,256]{2,1,0:T(8,128)(2,1)}), bf16[16,512,256]{2,1,0:T(8,128)(2,1)}, u32[]{:S(2)}, u32[]{:S(2)}) async-start(bf16[16,512,256]{2,1,0:T(8,128)(2,1)} %bitcast.90), calls=%async_computation | async-start | bytes 8388608 | tf_op jit(solution)/shard_map/all_to_all | solution.py:12
  32.9 1.0 fusion.23
  33.9 0.9 fusion.22
  35.8 0.6 gather_fusion
  36.5 179.9 %all-to-all-done = bf16[16,512,256]{2,1,0:T(8,128)(2,1)} async-done(((bf16[16,512,256]{2,1,0:T(8,128)(2,1)}), bf16[16,512,256]{2,1,0:T(8,128)(2,1)}, u32[]{:S(2)}, u32[]{:S(2)}) %all-to-all-start) | async-done | bytes 4194336 | tf_op jit(solution)/shard_map/all_to_all | solution.py:12
  216.5 2.8 gather_fusion.1
  219.4 12.6 %while.11 = (s32[]{:T(128)}, f32[4,4,128,256]{3,2,1,0:T(8,128)}, bf16[4,4,128,1024]{3,2,1,0:T(8,128)(2,1)}, bf16[4,4,8,256]{3,2,1,0:T(8,128)(2,1)S(1)}, bf16[4,4,128,256]{3,2,1,0:T(8,128)(2,1)S(1)}, /*index=5*/s32[]{:T(128)}) while((s32[]{:T(128)}, f32[4,4,128,256]{3,2,1,0:T(8,128)}, bf16[4,4,128,1024]{3,2,1,0:T(8,128)(2,1)}, ...), condition=%wide.region_7.8_spmd, body=%wide.region_6.7_spmd.sunk | while | flops 270671872 | bytes 7160909 | solution.py:46
  219.5 0.6 multiply_convert_fusion.2
  220.1 2.5 fusion.43
  222.7 0.6 multiply_convert_fusion.2
  223.3 2.5 fusion.43
  225.9 0.6 multiply_convert_fusion.2
  226.5 2.5 fusion.43
  229.0 0.6 multiply_convert_fusion.2
  229.6 2.5 fusion.43
  232.1 2.8 copy.13
  234.9 3.5 fusion.15
  238.4 4.9 reshape.83
  243.3 193.0 %all-reduce.6.cloned.1.call-done = f32[256,256]{0,1:T(8,128)} async-done(((f32[256,256]{0,1:T(8,128)}), f32[256,256]{0,1:T(8,128)}) %all-reduce.6.cloned.1.call-update) | async-done | bytes 262160 | tf_op jit(solution)/shard_map/psum | solution.py:70
  436.4 56.5 %all-reduce.4.cloned.1.call-done = f32[256,256]{0,1:T(8,128)} async-done(((f32[256,256]{0,1:T(8,128)}), f32[256,256]{0,1:T(8,128)}) %all-reduce.4.cloned.1.call-update) | async-done | bytes 262160 | tf_op jit(solution)/shard_map/psum | solution.py:71
  492.8 1.1 mul.24
  494.1 11.7 %cholesky.50 = f32[128,128]{1,0:T(8,128)S(1)} custom-call(f32[128,128]{1,0:T(8,128)S(1)} %cholesky.118), custom_call_target="Cholesky" | custom-call | tf_op jit(solution)/shard_map/jit(cholesky)/cholesky | solution.py:16
  505.9 9.8 %custom-call.16 = f32[1,128,128]{1,2,0:T(8,128)S(1)} custom-call(f32[1,128,128]{2,1,0:T(8,128)S(1)} %get-tuple-element.68), custom_call_target="InvertDiagBlocksLowerTriangular" | custom-call | tf_op jit(solution)/shard_map/jit(cholesky)/cholesky | solution.py:16
  515.7 0.2 constant_dynamic-update-slice_fusion.17
  515.9 0.3 convolution_subtract_fusion.2
  516.2 11.7 %cholesky.105 = f32[128,128]{1,0:T(8,128)S(1)} custom-call(f32[128,128]{1,0:T(8,128)S(1)} %convolution_subtract_fusion.2), custom_call_target="Cholesky" | custom-call | tf_op jit(solution)/shard_map/jit(cholesky)/cholesky | solution.py:16
  527.9 0.7 compare_reduce_fusion
  529.9 3.9 while.12
  530.0 0.6 fusion.44
  530.6 1.3 bitcast_dynamic-update-slice_fusion.2
  531.9 0.6 fusion.44
  532.5 1.3 bitcast_dynamic-update-slice_fusion.2
  533.9 19.9 %custom-call.17 = f32[2,128,128]{1,2,0:T(8,128)S(1)} custom-call(f32[2,128,128]{2,1,0:T(8,128)S(1)} %get-tuple-element.40), custom_call_target="InvertDiagBlocksLowerTriangular" | custom-call | tf_op jit(solution)/shard_map/triangular_solve | solution.py:18
  553.8 1.1 fusion.5
  554.9 1.1 convolution_subtract_fusion.1
  556.1 0.3 fusion.12
  556.4 0.2 fusion.11
  556.6 0.3 convolution_subtract_fusion
  557.1 0.8 copy.10
  (56 shorter events, 1.6 us)
Async XLA Ops:
  7.4 26.6 %copy-start = (bf16[16,256]{1,0:T(8,128)(2,1)S(1)}, bf16[16,256]{1,0:T(8,128)(2,1)}, u32[]{:S(2)}) copy-start(bf16[16,256]{1,0:T(8,128)(2,1)} %param.12) | copy-start | bytes 24580
  7.4 7.9 %copy-start.1 = (bf16[512,256]{1,0:T(8,128)(2,1)S(1)}, bf16[512,256]{1,0:T(8,128)(2,1)}, u32[]{:S(2)}) copy-start(bf16[512,256]{1,0:T(8,128)(2,1)} %param.13) | copy-start | bytes 786436
  15.5 2.0 copy-start.2
  17.4 17.5 %copy-start.4 = (s32[16,3]{0,1:T(4,128)S(1)}, s32[16,3]{0,1:T(4,128)}, u32[]{:S(2)}) copy-start(s32[16,3]{0,1:T(4,128)} %param.9) | copy-start | bytes 580
  17.4 199.0 %all-to-all-start = ((bf16[16,512,256]{2,1,0:T(8,128)(2,1)}), bf16[16,512,256]{2,1,0:T(8,128)(2,1)}, u32[]{:S(2)}, u32[]{:S(2)}) async-start(bf16[16,512,256]{2,1,0:T(8,128)(2,1)} %bitcast.90), calls=%async_computation | async-start | bytes 8388608 | tf_op jit(solution)/shard_map/all_to_all | solution.py:12
  32.8 403.5 %all-reduce.6.cloned.1.call-start = ((), (), s32[]{:S(2)}) async-start(), calls=%async_computation.3 | async-start | bytes 524288 | tf_op jit(solution)/shard_map/psum | solution.py:70
  33.9 459.0 %all-reduce.4.cloned.1.call-start = ((), (), s32[]{:S(2)}) async-start(), calls=%async_computation.2 | async-start | bytes 524288 | tf_op jit(solution)/shard_map/psum | solution.py:71
  34.9 518.9 %reduce-scatter.2.cloned.1.call-start = ((), (), s32[]{:S(2)}) async-start(), calls=%async_computation.4 | async-start | bytes 4325376 | tf_op jit(solution)/shard_map/reduce_scatter | solution.py:62
  232.1 2.8 copy-start.3
Sparse Core Ops, SparseCore 0:
  37.5 398.8 all-reduce.5
  438.8 54.0 all-reduce.3
Sparse Core Ops, SparseCore 1:
  243.4 104.5 reduce-scatter.1
